TPU v7x, 32 devices: a whole 2x2x4 slice. The times are simulated.
32 devices in a mesh: ctx: 8 (over y, x, core), qry: 4 (over z).
Axes of the slice: x: 2, y: 2, z: 4, core: 2. Of those that a mesh axis runs over, the one named last changes fastest.
Arguments:
- idx_query: bfloat16 [32, 8192], P('ctx', 'qry'), may hold values from -200 to 200
- idx_weight: bfloat16 [32, 64], P('ctx', 'qry'), may hold values from -3 to 3
- idx_keys: bfloat16 [16384, 128], P('ctx'), may hold values from -6 to 6
- q_latent: bfloat16 [32, 73728], P(('ctx', 'qry')), may hold values from -400 to 400
- latent_cache: bfloat16 [16384, 576], P('ctx'), may hold values from -20 to 20
- page_ids: int32 [32, 32], P(('ctx', 'qry')), may hold values from 0 to 255, as said below
Outputs:
- index_logp: float32 [32, 16384], P(('ctx', 'qry'))
- latent_out: bfloat16 [32, 65536], P(('ctx', 'qry'))
Inputs may be any that keep to these rules, and one draw needn't show every extreme that they name: `page_ids`: each row names 32 distinct pages, and no page id appears twice in the 1 row of one device (aligned blocks of 1 row). Page p holds tokens p * 64 to p * 64 + 63; ctx index j holds pages j * 32 to (j + 1) * 32 - 1. Of the 32 ids in the rows of one device, at most 8 lie on one ctx index, and in every such block some ctx index holds exactly 8.
All inputs are finite; a program needn't handle non-finite values.
Results may differ from a plain program's by a relative error of at most 0.013.
Values may be sent and summed in bfloat16 or wider, within the bound.
A program may use at most 64 MiB of HBM per device.

v0:
```python
import jax
import jax.numpy as jnp
from jax import lax
from jax.sharding import PartitionSpec as P

H_IDX = 64
D_IDX = 128
H = 128
D_LAT = 512
D_ROPE = 64
QK_NOPE = 128
PAGE = 64
TOPP = 32


def slot_ranks(requests, pages_dev):
    owner_shard = requests // pages_dev
    positions = jnp.arange(requests.shape[-1])
    earlier = positions[None, :] < positions[:, None]
    same_owner = owner_shard[..., :, None] == owner_shard[..., None, :]
    slot_rank = jnp.sum((same_owner & earlier).astype(jnp.int32), axis=-1)
    return (owner_shard, slot_rank)


def per_device(idx_query, idx_weight, idx_keys, q_latent, latent_cache, page_ids):
    shard_count = lax.axis_size("ctx")
    group_count = lax.axis_size("qry")
    ctx_index = lax.axis_index("ctx")
    rows_dev = q_latent.shape[0]
    ctx_dev = idx_keys.shape[0]
    latent_width = latent_cache.shape[1]
    pages_dev = ctx_dev // PAGE
    capacity = max(2, 2 * rows_dev * TOPP // shard_count)
    group_size = shard_count * rows_dev
    local_query = idx_query.reshape(group_count, rows_dev, idx_query.shape[1])
    local_weight = idx_weight.reshape(group_count, rows_dev, idx_weight.shape[1])
    every_query, every_weight = (
        lax.all_gather(local_query, "ctx", axis=0, tiled=True),
        lax.all_gather(local_weight, "ctx", axis=0, tiled=True),
    )
    group_query, group_weight = (
        lax.all_to_all(
            every_query.reshape(shard_count, group_count, rows_dev, idx_query.shape[1]),
            "qry",
            split_axis=1,
            concat_axis=3,
            tiled=True,
        ),
        lax.all_to_all(
            every_weight.reshape(shard_count, group_count, rows_dev, idx_weight.shape[1]),
            "qry",
            split_axis=1,
            concat_axis=3,
            tiled=True,
        ),
    )
    flat_query = group_query.reshape(group_size * H_IDX, D_IDX)
    head_weights = group_weight.reshape(group_size, H_IDX).astype(jnp.float32)
    block_width = min(512, ctx_dev)

    def score_block(step, table):
        key_block = lax.dynamic_slice_in_dim(idx_keys, step * block_width, block_width, 0)
        head_dots = lax.dot_general(
            flat_query, key_block, (((1,), (1,)), ((), ())), preferred_element_type=jnp.float32
        )
        active = jnp.maximum(head_dots, 0.0).reshape(group_size, H_IDX, block_width)
        summed = jnp.sum(active * head_weights[:, :, None], axis=1)
        return lax.dynamic_update_slice_in_dim(table, summed, step * block_width, 1)

    scores = lax.fori_loop(
        0, ctx_dev // block_width, score_block, jnp.zeros((group_size, ctx_dev), jnp.float32)
    )
    log_length = jnp.log(jnp.float32(ctx_dev * shard_count))
    score_table = lax.all_to_all(
        scores.astype(jnp.bfloat16), "ctx", split_axis=0, concat_axis=1, tiled=True
    ).astype(scores.dtype)
    row_max = jnp.max(score_table, axis=1, keepdims=True)
    row_total = jnp.sum(jnp.exp(score_table - row_max), axis=1, keepdims=True)
    index_logp = score_table - (row_max + jnp.log(row_total)) + log_length
    group_ids = lax.all_gather(page_ids, "ctx", axis=0, tiled=True)
    owner_shard, slot_rank = slot_ranks(group_ids, pages_dev)
    local_page = group_ids % pages_dev
    chosen = (owner_shard == ctx_index)[:, None, :] & (
        slot_rank[:, None, :] == jnp.arange(capacity)[None, :, None]
    )
    slot_page = jnp.sum(jnp.where(chosen, local_page[:, None, :], 0), axis=2)
    page_store = latent_cache.reshape(pages_dev, PAGE, latent_width)
    slot_keys = page_store[slot_page]
    logit_scale = (QK_NOPE + D_ROPE) ** (-0.5)
    arrived = lax.all_to_all(slot_keys, "ctx", split_axis=0, concat_axis=0, tiled=True)
    own_owner, own_rank = slot_ranks(page_ids.reshape(rows_dev * TOPP), pages_dev)
    slot_index = own_owner * capacity + own_rank
    key_rows = arrived.reshape(shard_count * capacity, PAGE, latent_width)[slot_index]
    key_rows = key_rows.reshape(rows_dev, TOPP * PAGE, latent_width)
    query_rows = q_latent.reshape(rows_dev, H, latent_width)
    logits = (
        jnp.einsum("qhd,qkd->qhk", query_rows, key_rows, preferred_element_type=jnp.float32)
        * logit_scale
    )
    logit_max = jnp.max(logits, axis=2, keepdims=True)
    expo = jnp.exp(logits - logit_max)
    att_weights = (expo / jnp.sum(expo, axis=2, keepdims=True)).astype(jnp.bfloat16)
    mixed_rows = jnp.einsum(
        "qhk,qkd->qhd", att_weights, key_rows[:, :, :D_LAT], preferred_element_type=jnp.float32
    )
    latent_out = mixed_rows.astype(jnp.bfloat16).reshape(rows_dev, H * D_LAT)
    return (index_logp, latent_out)


def solution(mesh):
    in_specs = (
        P("ctx", "qry"),
        P("ctx", "qry"),
        P("ctx", None),
        P(("ctx", "qry"), None),
        P("ctx", None),
        P(("ctx", "qry"), None),
    )
    out_specs = (P(("ctx", "qry"), None), P(("ctx", "qry"), None))
    return jax.shard_map(
        per_device, mesh=mesh, in_specs=in_specs, out_specs=out_specs, check_vma=False
    )
```

profile of v0, /device:TPU:0, one launch (start us, length us, event | category | flops | bytes accessed | tf_op | source)
XLA Modules:
  0.0 134.9 jit_solution(11475658209776853552)
XLA Ops:
  0.6 10.6 %all-gather.3 = bf16[8,4,16]{2,1,0:T(4,128)(2,1)S(1)} all-gather(bf16[1,4,16]{2,1,0:T(4,128)(2,1)} %bitcast.83), channel_id=3, replica_groups=mesh['ctx'=8,'qry'=4] {'ctx'}, dimensions={0}, use_global_device_ids=true | all-gather | bytes 1152 | tf_op jit(solution)/shard_map/all_gather | solution.py:39
  11.2 0.6 copy.20
  11.8 4.9 %all-to-all-start.1 = ((bf16[8,4,1,16]{3,0,2,1:T(8,128)(2,1)}), bf16[8,4,1,16]{3,0,2,1:T(8,128)(2,1)S(1)}, u32[]{:S(2)}, u32[]{:S(2)}) async-start(bf16[8,4,1,16]{3,0,2,1:T(8,128)(2,1)} %copy.20), calls=%async_computation.1 | async-start | bytes 16384 | tf_op jit(solution)/shard_map/all_to_all | solution.py:49
  16.7 8.6 %all-gather.4 = s32[8,1,32]{2,1,0:T(1,128)S(1)} all-gather(s32[1,1,32]{2,1,0:T(1,128)} %bitcast.84), channel_id=1, replica_groups=mesh['ctx'=8,'qry'=4] {'ctx'}, dimensions={0}, use_global_device_ids=true | all-gather | bytes 1152 | tf_op jit(solution)/shard_map/all_gather | solution.py:80
  25.3 0.3 convert_reduce_fusion
  25.6 0.2 select_reduce_fusion
  25.8 8.4 %all-gather.2 = bf16[8,4,2048]{2,1,0:T(4,128)(2,1)S(1)} all-gather(bf16[1,4,2048]{2,1,0:T(4,128)(2,1)} %bitcast.82), channel_id=2, replica_groups=mesh['ctx'=8,'qry'=4] {'ctx'}, dimensions={0}, use_global_device_ids=true | all-gather | bytes 147456 | tf_op jit(solution)/shard_map/all_gather | solution.py:38
  34.3 0.7 copy.18
  35.0 0.0 all-to-all-done.1
  35.0 5.1 %all-to-all-start = ((bf16[8,4,1,2048]{3,0,2,1:T(8,128)(2,1)}), bf16[8,4,1,2048]{3,0,2,1:T(8,128)(2,1)S(1)}, u32[]{:S(2)}, u32[]{:S(2)}) async-start(bf16[8,4,1,2048]{3,0,2,1:T(8,128)(2,1)} %copy.18), calls=%async_computation | async-start | bytes 262144 | tf_op jit(solution)/shard_map/all_to_all | solution.py:42
  40.1 0.1 reshape.281
  40.2 0.1 reshape.278
  40.2 6.3 %all-to-all-done = bf16[8,4,1,2048]{3,0,2,1:T(8,128)(2,1)S(1)} async-done(((bf16[8,4,1,2048]{3,0,2,1:T(8,128)(2,1)}), bf16[8,4,1,2048]{3,0,2,1:T(8,128)(2,1)S(1)}, u32[]{:S(2)}, u32[]{:S(2)}) %all-to-all-start) | async-done | bytes 131104 | tf_op jit(solution)/shard_map/all_to_all | solution.py:42
  46.5 0.1 copy.19
  46.6 0.1 reshape.266
  46.7 5.1 %while.13 = (s32[]{:T(128)}, bf16[8,2048]{1,0:T(8,128)(2,1)S(1)}, bf16[2048,128]{1,0:T(8,128)(2,1)}, bf16[512,128]{1,0:T(8,128)(2,1)S(1)}, f32[8,64]{1,0:T(8,128...) while((s32[]{:T(128)}, bf16[8,2048]{1,0:T(8,128)(2,1)S(1)}, bf16[2048,128]{1,0:T(8,128)(2,1)}, ...), condition=%wide.region_2.0_spmd, body=%wide.region_0.0_spmd.sunk | while | flops 67891208 | bytes 288915 | solution.py:70
  46.7 1.2 multiply_reduce_fusion.2
  48.0 1.2 multiply_reduce_fusion.2
  49.3 1.2 multiply_reduce_fusion.2
  50.5 1.2 multiply_reduce_fusion.2
  51.8 0.5 broadcast.203
  52.3 0.7 reduce.11
  53.0 0.6 reshape.309
  53.6 3.3 %all-to-all-start.2 = ((bf16[8,2,1024]{2,1,0:T(2,128)(2,1)}), bf16[8,2,1024]{2,1,0:T(2,128)(2,1)S(1)}, u32[]{:S(2)}, u32[]{:S(2)}) async-start(bf16[8,2,1024]{2,1,0:T(2,128)(2,1)} %reshape.309), calls=%async_computation.2 | async-start | bytes 65536 | tf_op jit(solution)/shard_map/all_to_all | solution.py:74
  57.0 3.1 %copy.23 = bf16[2048,576]{1,0:T(8,128)(2,1)S(1)} copy(bf16[2048,576]{0,1:T(8,128)(2,1)} %param.12) | data formatting | bytes 4718592 | tf_op args[4]
  60.1 3.5 %gather_fusion = bf16[64,64,576]{2,1,0:T(8,128)(2,1)} fusion(bf16[32,64,576]{2,1,0:T(8,128)(2,1)S(1)} %bitcast.71, s32[1024]{0:T(1024)S(1)} %pad_clamp_fusion.1), kind=kCustom, calls=%fused_computation | custom fusion | bytes 9437440 | tf_op jit(solution)/shard_map/gather | solution.py:88
  63.6 0.0 all-to-all-done.2
  63.6 0.0 copy-start
  63.6 0.0 copy-start.1
  63.6 4.8 %all-to-all-start.3 = ((bf16[8,8,64,576]{3,2,1,0:T(8,128)(2,1)}), bf16[8,8,64,576]{3,2,1,0:T(8,128)(2,1)}, u32[]{:S(2)}, u32[]{:S(2)}) async-start(bf16[8,8,64,576]{3,2,1,0:T(8,128)(2,1)} %bitcast.72), calls=%async_computation.3 | async-start | bytes 10485760 | tf_op jit(solution)/shard_map/all_to_all | solution.py:90
  68.4 0.0 copy-done
  68.4 0.9 reduce.10
  69.3 0.2 reshape.274
  69.4 0.0 copy-done.1
  69.5 0.2 convert_reduce_fusion.1
  69.7 0.7 reduce_max.23
  71.1 0.7 exponential_reduce_fusion
  73.2 0.7 subtract_add_fusion
  73.9 54.8 %all-to-all-done.3 = bf16[8,8,64,576]{3,2,1,0:T(8,128)(2,1)} async-done(((bf16[8,8,64,576]{3,2,1,0:T(8,128)(2,1)}), bf16[8,8,64,576]{3,2,1,0:T(8,128)(2,1)}, u32[]{:S(2)}, u32[]{:S(2)}) %all-to-all-start.3) | async-done | bytes 4718624 | tf_op jit(solution)/shard_map/all_to_all | solution.py:90
  128.7 3.5 %gather_fusion.1 = bf16[32,64,576]{2,1,0:T(8,128)(2,1)S(1)} fusion(bf16[64,64,576]{2,1,0:T(8,128)(2,1)} %bitcast.13, s32[1024]{0:T(1024)S(1)} %pad_clamp_fusion), kind=kCustom, calls=%fused_computation.1 | custom fusion | bytes 4718720 | tf_op jit(solution)/shard_map/gather | solution.py:93
  132.2 0.9 fusion.13
  133.1 0.3 fusion.5
  133.4 0.6 fusion.4
  134.0 0.9 copy.24
  (16 shorter events, 0.2 us)
Async XLA Ops:
  11.8 23.2 %all-to-all-start.1 = ((bf16[8,4,1,16]{3,0,2,1:T(8,128)(2,1)}), bf16[8,4,1,16]{3,0,2,1:T(8,128)(2,1)S(1)}, u32[]{:S(2)}, u32[]{:S(2)}) async-start(bf16[8,4,1,16]{3,0,2,1:T(8,128)(2,1)} %copy.20), calls=%async_computation.1 | async-start | bytes 16384 | tf_op jit(solution)/shard_map/all_to_all | solution.py:49
  35.0 11.5 %all-to-all-start = ((bf16[8,4,1,2048]{3,0,2,1:T(8,128)(2,1)}), bf16[8,4,1,2048]{3,0,2,1:T(8,128)(2,1)S(1)}, u32[]{:S(2)}, u32[]{:S(2)}) async-start(bf16[8,4,1,2048]{3,0,2,1:T(8,128)(2,1)} %copy.18), calls=%async_computation | async-start | bytes 262144 | tf_op jit(solution)/shard_map/all_to_all | solution.py:42
  53.6 10.0 %all-to-all-start.2 = ((bf16[8,2,1024]{2,1,0:T(2,128)(2,1)}), bf16[8,2,1024]{2,1,0:T(2,128)(2,1)S(1)}, u32[]{:S(2)}, u32[]{:S(2)}) async-start(bf16[8,2,1024]{2,1,0:T(2,128)(2,1)} %reshape.309), calls=%async_computation.2 | async-start | bytes 65536 | tf_op jit(solution)/shard_map/all_to_all | solution.py:74
  63.6 4.8 %copy-start = (bf16[1,73728]{1,0:T(2,128)(2,1)S(1)}, bf16[1,73728]{1,0:T(2,128)(2,1)}, u32[]{:S(2)}) copy-start(bf16[1,73728]{1,0:T(2,128)(2,1)} %param.11) | copy-start | bytes 442372
  63.6 5.8 %copy-start.1 = (s32[1,32]{1,0:T(1,128)S(1)}, s32[1,32]{1,0:T(1,128)}, u32[]{:S(2)}) copy-start(s32[1,32]{1,0:T(1,128)} %param.13) | copy-start | bytes 388
  63.6 65.1 %all-to-all-start.3 = ((bf16[8,8,64,576]{3,2,1,0:T(8,128)(2,1)}), bf16[8,8,64,576]{3,2,1,0:T(8,128)(2,1)}, u32[]{:S(2)}, u32[]{:S(2)}) async-start(bf16[8,8,64,576]{3,2,1,0:T(8,128)(2,1)} %bitcast.72), calls=%async_computation.3 | async-start | bytes 10485760 | tf_op jit(solution)/shard_map/all_to_all | solution.py:90
where the time goes:
time: 136 us; the launch traced here: 135 us
  waiting for transfers between devices  61.1 us (45%)
  blocking collectives  27.6 us (20%)
  starting transfers between devices  18.1 us (13%)
  local copies, waits for them, and re-layouts  14.1 us (10%)
  matrix products  6.35 us (5%)
  other arithmetic  4.78 us (4%)
  between operations  2.79 us (2%)
    all_to_all x1, waiting for transfers between devices, per_device(): lax.all_to_all(slot_keys, 'ctx', split_axis=0, concat_axis=0, tiled=True)  54.8 us
    all_gather x1, blocking collectives, per_device(): lax.all_gather(local_weight, 'ctx', axis=0, tiled=True)  10.6 us
    all_gather x1, blocking collectives, per_device(): group_ids = lax.all_gather(page_ids, 'ctx', axis=0, tiled=True)  8.63 us
    all_gather x1, blocking collectives, per_device(): lax.all_gather(local_query, 'ctx', axis=0, tiled=True)  8.42 us
    all_to_all x1, waiting for transfers between devices, per_device(): lax.all_to_all(every_query.reshape(shard_count, group_count, rows_dev, id...  6.25 us
    all_to_all x1, starting transfers between devices, per_device(): lax.all_to_all(every_query.reshape(shard_count, group_count, rows_dev, id...  5.07 us
    dot_general x4, matrix products, score_block(): lax.dot_general(flat_query, key_block, (((1,), (1,)), ((), ())), preferre...  4.91 us
    all_to_all x1, starting transfers between devices, per_device(): lax.all_to_all(every_weight.reshape(shard_count, group_count, rows_dev, i...  4.87 us
  transfers between devices with their start and end apart: 4, of which 2 were waited for; matrix products, arithmetic and copies ran while one was open for 9% of the time, Pallas kernels for 0%

commit v1 on v0

--- a/solution.py
+++ b/solution.py
@@ -2,6 +2,7 @@
 import jax.numpy as jnp
 from jax import lax
 from jax.sharding import PartitionSpec as P
+from jax.lax import axis_index, axis_size, ppermute
 
 H_IDX = 64
 D_IDX = 128
@@ -87,7 +88,25 @@
     page_store = latent_cache.reshape(pages_dev, PAGE, latent_width)
     slot_keys = page_store[slot_page]
     logit_scale = (QK_NOPE + D_ROPE) ** (-0.5)
-    arrived = lax.all_to_all(slot_keys, "ctx", split_axis=0, concat_axis=0, tiled=True)
+    w1 = axis_size("ctx")
+    x_now = axis_index("ctx")
+    u_next, p_next = (w1, x_now)
+    back = slot_keys.shape[0] // u_next
+    mid_arr = jnp.roll(slot_keys, -p_next * back, 0)
+    known = lax.slice_in_dim(mid_arr, 0, back, axis=0)
+    line_up = [known]
+    num = 1
+    while num < u_next:
+        r1 = lax.slice_in_dim(mid_arr, num * back, (num + 1) * back, axis=0)
+        line_up.append(
+            ppermute(
+                r1, axis_name="ctx", perm=[(nth, (nth + num) % u_next) for nth in range(u_next)]
+            )
+        )
+        num = num + 1
+    arrived = jnp.roll(
+        jnp.concatenate(line_up[::-1], axis=0), (p_next + 1) * line_up[0].shape[0], axis=0
+    )
     own_owner, own_rank = slot_ranks(page_ids.reshape(rows_dev * TOPP), pages_dev)
     slot_index = own_owner * capacity + own_rank
     key_rows = arrived.reshape(shard_count * capacity, PAGE, latent_width)[slot_index]

time: 136 us -> 174 us (1.28)
  blocking collectives: 27.6 us -> 78 us
  waiting for transfers between devices: 61.1 us -> 25.9 us
  local copies, waits for them, and re-layouts: 14.1 us -> 25.8 us
  other arithmetic: 4.78 us -> 15 us
    all_to_all x1 -> x0, waiting for transfers between devices: 54.8 us -> none  [per_device(): lax.all_to_all(slot_keys, 'ctx', split_axis=0, concat_axis=0, tiled=True)]
    all_gather x1, blocking collectives: 10.6 us -> 59.3 us  [per_device(): lax.all_gather(local_weight, 'ctx', axis=0, tiled=True)]
    ppermute x0 -> x7, waiting for transfers between devices: none -> 17.5 us  [per_device(): ppermute(r1, axis_name='ctx', perm=[(nth, (nth + num) % u_next) for nth i...]
    concatenate x0 -> x2, other arithmetic: none -> 9.35 us  [the longest x1 4.75 us: per_device(): mid_arr = jnp.roll(slot_keys, -p_next * back, 0)]
    unnamed x8 -> x21, local copies, waits for them, and re-layouts: 4.66 us -> 13 us
    ppermute x0 -> x7, starting transfers between devices: none -> 5.67 us  [per_device(): ppermute(r1, axis_name='ctx', perm=[(nth, (nth + num) % u_next) for nth i...]
    all_to_all x1 -> x0, starting transfers between devices: 4.78 us -> none  [per_device(): lax.all_to_all(slot_keys, 'ctx', split_axis=0, concat_axis=0, tiled=True)]
    all_to_all x1, waiting for transfers between devices: 0.01 us -> 2.14 us  [per_device(): lax.all_to_all(scores.astype(jnp.bfloat16), 'ctx', split_axis=0, concat_a...]
  transfers between devices with their start and end apart: 4 -> 10, of which waited for: 2 -> 4; matrix products, arithmetic and copies ran while one was open for 9% -> 11% of each run, Pallas kernels for 0% -> 0%
where the time goes in v1:
time: 174 us; the launch traced here: 173 us
  blocking collectives  78 us (45%)
  waiting for transfers between devices  25.9 us (15%)
  local copies, waits for them, and re-layouts  25.8 us (15%)
  starting transfers between devices  19 us (11%)
  other arithmetic  15 us (9%)
  matrix products  6.35 us (4%)
  between operations  2.86 us (2%)
    all_gather x1, blocking collectives, per_device(): lax.all_gather(local_weight, 'ctx', axis=0, tiled=True)  59.3 us
    ppermute x7, waiting for transfers between devices, per_device(): ppermute(r1, axis_name='ctx', perm=[(nth, (nth + num) % u_next) for nth i...  17.5 us
    unnamed x21, local copies, waits for them, and re-layouts  13 us
    all_gather x1, blocking collectives, per_device(): group_ids = lax.all_gather(page_ids, 'ctx', axis=0, tiled=True)  10.4 us
    all_gather x1, blocking collectives, per_device(): lax.all_gather(local_query, 'ctx', axis=0, tiled=True)  8.25 us
    all_to_all x1, waiting for transfers between devices, per_device(): lax.all_to_all(every_query.reshape(shard_count, group_count, rows_dev, id...  6.32 us
    ppermute x7, starting transfers between devices, per_device(): ppermute(r1, axis_name='ctx', perm=[(nth, (nth + num) % u_next) for nth i...  5.67 us
    all_to_all x1, starting transfers between devices, per_device(): lax.all_to_all(every_query.reshape(shard_count, group_count, rows_dev, id...  5.09 us
  transfers between devices with their start and end apart: 10, of which 4 were waited for; matrix products, arithmetic and copies ran while one was open for 11% of the time, Pallas kernels for 0%

profile of v1, /device:TPU:0, one launch (start us, length us, event | category | flops | bytes accessed | tf_op | source)
XLA Modules:
  0.0 173.1 jit_solution(7367100711462379652)
XLA Ops:
  0.7 10.4 %all-gather.4 = s32[8,1,32]{2,1,0:T(1,128)S(1)} all-gather(s32[1,1,32]{2,1,0:T(1,128)} %bitcast.85), channel_id=1, replica_groups=mesh['ctx'=8,'qry'=4] {'ctx'}, dimensions={0}, use_global_device_ids=true | all-gather | bytes 1152 | tf_op jit(solution)/shard_map/all_gather | solution.py:81
  11.1 0.3 convert_reduce_fusion
  11.4 0.2 select_reduce_fusion
  11.6 0.1 reshape.281
  11.7 3.1 %copy.23 = bf16[2048,576]{1,0:T(8,128)(2,1)S(1)} copy(bf16[2048,576]{0,1:T(8,128)(2,1)} %param.14) | data formatting | bytes 4718592 | tf_op args[4]
  14.8 3.5 %gather_fusion = bf16[64,64,576]{2,1,0:T(8,128)(2,1)} fusion(bf16[32,64,576]{2,1,0:T(8,128)(2,1)S(1)} %bitcast.71, s32[1024]{0:T(1024)S(1)} %pad_clamp_fusion.1), kind=kCustom, calls=%fused_computation | custom fusion | bytes 9437440 | tf_op jit(solution)/shard_map/gather | solution.py:89
  18.3 4.8 %fusion.3 = bf16[8,8,64,576]{3,2,1,0:T(8,128)(2,1)S(1)} fusion(s32[]{:T(128)S(6)} %select_n.84, bf16[8,8,64,576]{3,2,1,0:T(8,128)(2,1)} %bitcast.72), kind=kLoop, calls=%fused_computation.12 | loop fusion | flops 2359296 | bytes 9437188 | tf_op jit(solution)/shard_map/jit(_roll_dynamic)/concatenate | solution.py:95
  23.1 2.3 %copy-done = bf16[8,8,64,576]{3,2,1,0:T(8,128)(2,1)} copy-done((bf16[8,8,64,576]{3,2,1,0:T(8,128)(2,1)}, bf16[8,8,64,576]{3,2,1,0:T(8,128)(2,1)S(1)}, u32[]{:S(2)}) %copy-start) | copy-done | bytes 4718616
  25.4 1.5 fusion.15
  26.9 1.3 collective-permute-start
  28.2 1.5 collective-permute-start.1
  29.7 0.0 collective-permute-start.2
  29.7 0.6 collective-permute-start.3
  30.3 1.5 collective-permute-start.4
  31.8 59.3 %all-gather.3 = bf16[8,4,16]{2,1,0:T(4,128)(2,1)S(1)} all-gather(bf16[1,4,16]{2,1,0:T(4,128)(2,1)S(1)} %bitcast.84), channel_id=3, replica_groups=mesh['ctx'=8,'qry'=4] {'ctx'}, dimensions={0}, use_global_device_ids=true | all-gather | bytes 1152 | tf_op jit(solution)/shard_map/all_gather | solution.py:40
  91.1 0.6 copy.20
  91.8 4.9 %all-to-all-start.1 = ((bf16[8,4,1,16]{3,0,2,1:T(8,128)(2,1)}), bf16[8,4,1,16]{3,0,2,1:T(8,128)(2,1)S(1)}, u32[]{:S(2)}, u32[]{:S(2)}) async-start(bf16[8,4,1,16]{3,0,2,1:T(8,128)(2,1)} %copy.20), calls=%async_computation.1 | async-start | bytes 16384 | tf_op jit(solution)/shard_map/all_to_all | solution.py:50
  96.7 0.2 convert_reduce_fusion.1
  96.8 8.2 %all-gather.2 = bf16[8,4,2048]{2,1,0:T(4,128)(2,1)S(1)} all-gather(bf16[1,4,2048]{2,1,0:T(4,128)(2,1)S(1)} %bitcast.83), channel_id=2, replica_groups=mesh['ctx'=8,'qry'=4] {'ctx'}, dimensions={0}, use_global_device_ids=true | all-gather | bytes 147456 | tf_op jit(solution)/shard_map/all_gather | solution.py:39
  105.1 0.7 copy.18
  105.8 0.0 all-to-all-done.1
  105.8 5.1 %all-to-all-start = ((bf16[8,4,1,2048]{3,0,2,1:T(8,128)(2,1)}), bf16[8,4,1,2048]{3,0,2,1:T(8,128)(2,1)S(1)}, u32[]{:S(2)}, u32[]{:S(2)}) async-start(bf16[8,4,1,2048]{3,0,2,1:T(8,128)(2,1)} %copy.18), calls=%async_computation | async-start | bytes 262144 | tf_op jit(solution)/shard_map/all_to_all | solution.py:43
  110.9 0.1 reshape.278
  111.0 6.3 %all-to-all-done = bf16[8,4,1,2048]{3,0,2,1:T(8,128)(2,1)S(1)} async-done(((bf16[8,4,1,2048]{3,0,2,1:T(8,128)(2,1)}), bf16[8,4,1,2048]{3,0,2,1:T(8,128)(2,1)S(1)}, u32[]{:S(2)}, u32[]{:S(2)}) %all-to-all-start) | async-done | bytes 131104 | tf_op jit(solution)/shard_map/all_to_all | solution.py:43
  117.3 0.1 copy.19
  117.4 0.1 reshape.266
  117.6 5.1 %while.13 = (s32[]{:T(128)}, bf16[8,2048]{1,0:T(8,128)(2,1)S(1)}, bf16[2048,128]{1,0:T(8,128)(2,1)}, bf16[512,128]{1,0:T(8,128)(2,1)S(1)}, f32[8,64]{1,0:T(8,128...) while((s32[]{:T(128)}, bf16[8,2048]{1,0:T(8,128)(2,1)S(1)}, bf16[2048,128]{1,0:T(8,128)(2,1)}, ...), condition=%wide.region_2.0_spmd, body=%wide.region_0.0_spmd.sunk | while | flops 67891208 | bytes 288915 | solution.py:71
  117.6 1.2 multiply_reduce_fusion.2
  118.8 1.2 multiply_reduce_fusion.2
  120.1 1.2 multiply_reduce_fusion.2
  121.4 1.2 multiply_reduce_fusion.2
  122.6 0.5 broadcast.221
  123.1 0.7 reduce.11
  123.8 0.6 reshape.309
  124.4 3.3 %all-to-all-start.2 = ((bf16[8,2,1024]{2,1,0:T(2,128)(2,1)}), bf16[8,2,1024]{2,1,0:T(2,128)(2,1)S(1)}, u32[]{:S(2)}, u32[]{:S(2)}) async-start(bf16[8,2,1024]{2,1,0:T(2,128)(2,1)} %reshape.309), calls=%async_computation.2 | async-start | bytes 65536 | tf_op jit(solution)/shard_map/all_to_all | solution.py:75
  127.8 1.8 %reduce.10 = bf16[73728]{0:T(1024)(128)(2,1)S(1)} reduce(bf16[1,73728]{1,0:T(2,128)(2,1)} %param.13, bf16[]{:T(256)} %constant.119), dimensions={0}, to_apply=%param.13.reduce_sub_computation | reduce | bytes 294914 | tf_op args[3]
  129.6 0.8 reshape.274
  130.4 2.1 %all-to-all-done.2 = bf16[8,2,1024]{2,1,0:T(2,128)(2,1)S(1)} async-done(((bf16[8,2,1024]{2,1,0:T(2,128)(2,1)}), bf16[8,2,1024]{2,1,0:T(2,128)(2,1)S(1)}, u32[]{:S(2)}, u32[]{:S(2)}) %all-to-all-start.2) | async-done | bytes 32800 | tf_op jit(solution)/shard_map/all_to_all | solution.py:75
  132.6 0.7 reduce_max.23
  134.0 0.8 exponential_reduce_fusion
  136.0 0.7 subtract_add_fusion
  136.7 0.0 collective-permute-done
  136.7 0.6 collective-permute-start.5
  137.3 1.1 constant_dynamic-update-slice_fusion.7
  138.4 0.0 collective-permute-done.1
  138.4 0.2 collective-permute-start.6
  138.7 1.2 constant_dynamic-update-slice_fusion.6
  139.9 0.0 collective-permute-done.2
  139.9 1.2 constant_dynamic-update-slice_fusion.5
  141.1 0.0 collective-permute-done.3
  141.1 1.2 constant_dynamic-update-slice_fusion.4
  142.3 0.0 collective-permute-done.4
  142.3 1.2 constant_dynamic-update-slice_fusion.3
  143.5 11.8 %collective-permute-done.5 = bf16[1,8,64,576]{3,2,1,0:T(8,128)(2,1)S(1)} collective-permute-done((bf16[1,8,64,576]{3,2,1,0:T(8,128)(2,1)S(1)}, bf16[1,8,64,576]{3,2,1,0:T(8,128)(2,1)S(1)}, u32[]{:S(2)}, u32[]{:S(2)}) %collective-permute-start.5) | collective-permute-done | bytes 589856 | tf_op jit(solution)/shard_map/ppermute | solution.py:102
  155.2 0.1 constant_dynamic-update-slice_fusion.2
  155.3 5.7 %collective-permute-done.6 = bf16[1,8,64,576]{3,2,1,0:T(8,128)(2,1)S(1)} collective-permute-done((bf16[1,8,64,576]{3,2,1,0:T(8,128)(2,1)S(1)}, bf16[1,8,64,576]{3,2,1,0:T(8,128)(2,1)S(1)}, u32[]{:S(2)}, u32[]{:S(2)}) %collective-permute-start.6) | collective-permute-done | bytes 589856 | tf_op jit(solution)/shard_map/ppermute | solution.py:102
  161.0 0.1 constant_dynamic-update-slice_fusion.1
  161.1 1.2 slice_dynamic-update-slice_fusion
  162.3 4.6 %fusion.2 = bf16[8,8,64,576]{3,2,1,0:T(8,128)(2,1)} fusion(s32[]{:T(128)S(6)} %select_n.86, bf16[8,8,64,576]{3,2,1,0:T(8,128)(2,1)S(1)} %slice_dynamic-update-slice_fusion), kind=kLoop, calls=%fused_computation.11 | loop fusion | flops 2359296 | bytes 9437188 | tf_op jit(solution)/shard_map/jit(_roll_dynamic)/concatenate | solution.py:107
  166.9 3.5 %gather_fusion.1 = bf16[32,64,576]{2,1,0:T(8,128)(2,1)S(1)} fusion(bf16[64,64,576]{2,1,0:T(8,128)(2,1)} %bitcast.73, s32[1024]{0:T(1024)S(1)} %pad_clamp_fusion), kind=kCustom, calls=%fused_computation.1 | custom fusion | bytes 4718720 | tf_op jit(solution)/shard_map/gather | solution.py:112
  170.5 0.9 fusion.16
  171.3 0.3 fusion.7
  171.6 0.6 fusion.6
  172.2 0.9 copy.24
  (25 shorter events, 0.2 us)
Async XLA Ops:
  23.1 2.3 %copy-start = (bf16[8,8,64,576]{3,2,1,0:T(8,128)(2,1)}, bf16[8,8,64,576]{3,2,1,0:T(8,128)(2,1)S(1)}, u32[]{:S(2)}) copy-start(bf16[8,8,64,576]{3,2,1,0:T(8,128)(2,1)S(1)} %fusion.3) | copy-start | bytes 14155780
  25.4 6.4 %copy-start.3 = (bf16[4,16]{1,0:T(4,128)(2,1)S(1)}, bf16[4,16]{1,0:T(4,128)(2,1)}, u32[]{:S(2)}) copy-start(bf16[4,16]{1,0:T(4,128)(2,1)} %param.11) | copy-start | bytes 388
  25.4 71.2 %copy-start.4 = (s32[1,32]{1,0:T(1,128)S(1)}, s32[1,32]{1,0:T(1,128)}, u32[]{:S(2)}) copy-start(s32[1,32]{1,0:T(1,128)} %param.15) | copy-start | bytes 388
  25.4 71.5 %copy-start.2 = (bf16[4,2048]{1,0:T(4,128)(2,1)S(1)}, bf16[4,2048]{1,0:T(4,128)(2,1)}, u32[]{:S(2)}) copy-start(bf16[4,2048]{1,0:T(4,128)(2,1)} %param.10) | copy-start | bytes 49156
  26.9 109.8 %collective-permute-start = (bf16[1,8,64,576]{3,2,1,0:T(8,128)(2,1)}, bf16[1,8,64,576]{3,2,1,0:T(8,128)(2,1)}, u32[]{:S(2)}, u32[]{:S(2)}) collective-permute-start(bf16[1,8,64,576]{3,2,1,0:T(8,128)(2,1)} %get-tuple-element.116), channel_id=1, source_target_pairs={{0,28},{4,0},{8,4},{12,8},{16,12},{20,16},{24,20},{28,24},{1,29},{... | collective-permute-start | bytes 1769480 | tf_op jit(solution)/shard_map/ppermute | solution.py:102
  28.2 110.2 %collective-permute-start.1 = (bf16[1,8,64,576]{3,2,1,0:T(8,128)(2,1)}, bf16[1,8,64,576]{3,2,1,0:T(8,128)(2,1)}, u32[]{:S(2)}, u32[]{:S(2)}) collective-permute-start(bf16[1,8,64,576]{3,2,1,0:T(8,128)(2,1)} %get-tuple-element.115), channel_id=1, source_target_pairs={{0,24},{4,28},{8,0},{12,4},{16,8},{20,12},{24,16},{28,20},{1,25},{... | collective-permute-start | bytes 1769480 | tf_op jit(solution)/shard_map/ppermute | solution.py:102
  29.7 110.1 %collective-permute-start.2 = (bf16[1,8,64,576]{3,2,1,0:T(8,128)(2,1)S(1)}, bf16[1,8,64,576]{3,2,1,0:T(8,128)(2,1)}, u32[]{:S(2)}, u32[]{:S(2)}) collective-permute-start(bf16[1,8,64,576]{3,2,1,0:T(8,128)(2,1)S(1)} %get-tuple-element.114), channel_id=1, source_target_pairs={{0,20},{4,24},{8,28},{12,0},{16,4},{20,8},{24,12},{28,16},{1,21},{... | collective-permute-start | bytes 1769480 | tf_op jit(solution)/shard_map/ppermute | solution.py:102
  29.7 111.3 %collective-permute-start.3 = (bf16[1,8,64,576]{3,2,1,0:T(8,128)(2,1)S(1)}, bf16[1,8,64,576]{3,2,1,0:T(8,128)(2,1)}, u32[]{:S(2)}, u32[]{:S(2)}) collective-permute-start(bf16[1,8,64,576]{3,2,1,0:T(8,128)(2,1)S(1)} %get-tuple-element.113), channel_id=1, source_target_pairs={{0,16},{4,20},{8,24},{12,28},{16,0},{20,4},{24,8},{28,12},{1,17},{... | collective-permute-start | bytes 1769480 | tf_op jit(solution)/shard_map/ppermute | solution.py:102
  30.3 111.9 %collective-permute-start.4 = (bf16[1,8,64,576]{3,2,1,0:T(8,128)(2,1)S(1)}, bf16[1,8,64,576]{3,2,1,0:T(8,128)(2,1)}, u32[]{:S(2)}, u32[]{:S(2)}) collective-permute-start(bf16[1,8,64,576]{3,2,1,0:T(8,128)(2,1)S(1)} %get-tuple-element.112), channel_id=1, source_target_pairs={{0,12},{4,16},{8,20},{12,24},{16,28},{20,0},{24,4},{28,8},{1,13},{... | collective-permute-start | bytes 1769480 | tf_op jit(solution)/shard_map/ppermute | solution.py:102
  91.8 14.1 %all-to-all-start.1 = ((bf16[8,4,1,16]{3,0,2,1:T(8,128)(2,1)}), bf16[8,4,1,16]{3,0,2,1:T(8,128)(2,1)S(1)}, u32[]{:S(2)}, u32[]{:S(2)}) async-start(bf16[8,4,1,16]{3,0,2,1:T(8,128)(2,1)} %copy.20), calls=%async_computation.1 | async-start | bytes 16384 | tf_op jit(solution)/shard_map/all_to_all | solution.py:50
  105.8 11.5 %all-to-all-start = ((bf16[8,4,1,2048]{3,0,2,1:T(8,128)(2,1)}), bf16[8,4,1,2048]{3,0,2,1:T(8,128)(2,1)S(1)}, u32[]{:S(2)}, u32[]{:S(2)}) async-start(bf16[8,4,1,2048]{3,0,2,1:T(8,128)(2,1)} %copy.18), calls=%async_computation | async-start | bytes 262144 | tf_op jit(solution)/shard_map/all_to_all | solution.py:43
  124.4 8.1 %all-to-all-start.2 = ((bf16[8,2,1024]{2,1,0:T(2,128)(2,1)}), bf16[8,2,1024]{2,1,0:T(2,128)(2,1)S(1)}, u32[]{:S(2)}, u32[]{:S(2)}) async-start(bf16[8,2,1024]{2,1,0:T(2,128)(2,1)} %reshape.309), calls=%async_computation.2 | async-start | bytes 65536 | tf_op jit(solution)/shard_map/all_to_all | solution.py:75
  136.7 18.5 %collective-permute-start.5 = (bf16[1,8,64,576]{3,2,1,0:T(8,128)(2,1)S(1)}, bf16[1,8,64,576]{3,2,1,0:T(8,128)(2,1)S(1)}, u32[]{:S(2)}, u32[]{:S(2)}) collective-permute-start(bf16[1,8,64,576]{3,2,1,0:T(8,128)(2,1)S(1)} %get-tuple-element.111), channel_id=1, source_target_pairs={{0,8},{4,12},{8,16},{12,20},{16,24},{20,28},{24,0},{28,4},{1,9},{5... | collective-permute-start | bytes 1769480 | tf_op jit(solution)/shard_map/ppermute | solution.py:102
  138.4 22.6 %collective-permute-start.6 = (bf16[1,8,64,576]{3,2,1,0:T(8,128)(2,1)S(1)}, bf16[1,8,64,576]{3,2,1,0:T(8,128)(2,1)S(1)}, u32[]{:S(2)}, u32[]{:S(2)}) collective-permute-start(bf16[1,8,64,576]{3,2,1,0:T(8,128)(2,1)S(1)} %get-tuple-element.110), channel_id=1, source_target_pairs={{0,4},{4,8},{8,12},{12,16},{16,20},{20,24},{24,28},{28,0},{1,5},{5... | collective-permute-start | bytes 1769480 | tf_op jit(solution)/shard_map/ppermute | solution.py:102
  166.9 3.6 %copy-start.1 = (bf16[128,576]{1,0:T(8,128)(2,1)S(1)}, bf16[128,576]{1,0:T(8,128)(2,1)}, u32[]{:S(2)}) copy-start(bf16[128,576]{1,0:T(8,128)(2,1)} %reshape.274) | copy-start | bytes 442372
